TPU v7x, 256 devices: a whole 4x4x8 slice. The times are simulated.
256 devices in a mesh: rows: 32 (over z, y), cols: 8 (over x, core).
Axes of the slice: x: 4, y: 4, z: 8, core: 2. Of those that a mesh axis runs over, the one named last changes fastest.
Arguments:
- features: float32 [32768, 4, 8, 256], P('rows', None, 'cols'), may hold values from -6 to 6
Outputs:
- factor_rows: float32 [512, 4, 8, 256], P(None, None, 'cols')
- basis: float32 [32768, 2, 256], P('rows')
- trailing: float32 [32768, 4, 8, 256], P('rows', None, 'cols')
All inputs are finite; a program needn't handle non-finite values.
Results may differ from a plain program's by a relative error of at most 0.0003.
Values sent between devices are 32-bit elements; how exact they have to be, the bound alone decides.
A program may use at most 64 MiB of HBM per device.

v0:
```python
import jax
import jax.numpy as jnp
from jax import lax
from jax.sharding import PartitionSpec as P

HIGHEST = lax.Precision.HIGHEST


def broadcast(array, axis, root):
    mine = lax.axis_index(axis) == root
    return lax.psum(jnp.where(mine, array, jnp.zeros_like(array)), axis)


def product(left, right):
    return jnp.dot(left, right, precision=HIGHEST)


def lower_solve(gram, panel):
    lower = jnp.linalg.cholesky(gram)
    solved = lax.linalg.triangular_solve(lower, panel.T, left_side=True, lower=True).T
    return (solved, lower)


def single_pass(panel):
    gram = lax.psum(product(panel.T, panel), "rows")
    return lower_solve(gram, panel)[0]


def send_basis(basis, owner):
    return broadcast(basis, "cols", owner)


def panel_basis(panel, owner):
    return send_basis(single_pass(panel), owner)


def factor_project(panel, owner, block):
    basis = panel_basis(panel, owner)
    return (basis, lax.psum(product(basis.T, block), "rows"))


def on_device(features):
    rows_dev = features.shape[0]
    pan_dev = features.shape[1]
    width = features.shape[3]
    local = features.reshape(rows_dev, pan_dev * width)
    first_cols = local[:, :width]
    basis_a, proj_a = factor_project(first_cols, 0, local)
    updated = local - product(basis_a, proj_a)
    basis_b, proj_b = factor_project(updated[:, :width], 1, updated)
    final = updated - product(basis_b, proj_b)
    factor_rows = jnp.concatenate([proj_a, proj_b], axis=0).reshape(2 * width, pan_dev, 1, width)
    basis = jnp.stack([basis_a, basis_b], axis=1)
    return (factor_rows, basis, final.reshape(rows_dev, pan_dev, 1, width))


def solution(mesh):
    placed = (P("rows", None, "cols", None),)
    return jax.shard_map(
        on_device,
        mesh=mesh,
        in_specs=placed,
        out_specs=(
            P(None, None, "cols", None),
            P("rows", None, None),
            P("rows", None, "cols", None),
        ),
        check_vma=False,
    )
```

profile of v0, /device:TPU:1, one launch (start us, length us, event | category | flops | bytes accessed | tf_op | source)
XLA Modules:
  0.0 922.6 jit_solution(8131912290005382858)
XLA Ops:
  7.2 10.9 %copy.4 = f32[1024,4,1,256]{0,3,1,2:T(8,128)} copy(f32[1024,4,1,256]{3,2,1,0:T(1,128)} %param.4) | data formatting | bytes 8388608 | tf_op args[0]
  18.1 3.4 fusion.4
  21.6 1.3 slice_bitcast_fusion.1
  22.9 142.3 %all-reduce.8.cloned.1.call-done = f32[256,256]{0,1:T(8,128)} async-done(((f32[256,256]{0,1:T(8,128)}), f32[256,256]{0,1:T(8,128)}) %all-reduce.8.cloned.1.call-update) | async-done | bytes 262160 | tf_op jit(solution)/shard_map/psum | solution.py:25
  165.2 1.1 copy.6
  166.3 1.0 fusion.11
  167.3 11.7 %cholesky.130 = f32[128,128]{1,0:T(8,128)S(1)} custom-call(f32[128,128]{1,0:T(8,128)S(1)} %cholesky.194), custom_call_target="Cholesky" | custom-call | tf_op jit(solution)/shard_map/jit(cholesky)/cholesky | solution.py:19
  179.0 9.8 %custom-call.13 = f32[1,128,128]{1,2,0:T(8,128)S(1)} custom-call(f32[1,128,128]{2,1,0:T(8,128)S(1)} %get-tuple-element.51), custom_call_target="InvertDiagBlocksLowerTriangular" | custom-call | tf_op jit(solution)/shard_map/jit(cholesky)/cholesky | solution.py:19
  189.4 11.7 %cholesky.147 = f32[128,128]{1,0:T(8,128)S(1)} custom-call(f32[128,128]{1,0:T(8,128)S(1)} %convolution_subtract_fusion.5), custom_call_target="Cholesky" | custom-call | tf_op jit(solution)/shard_map/jit(cholesky)/cholesky | solution.py:19
  201.1 0.7 compare_reduce_fusion.2
  203.3 4.6 while.4
  204.4 1.4 bitcast_dynamic-update-slice_fusion.4
  206.4 1.4 bitcast_dynamic-update-slice_fusion.4
  207.9 19.7 %custom-call.14 = f32[2,128,128]{1,2,0:T(8,128)S(1)} custom-call(f32[2,128,128]{2,1,0:T(8,128)S(1)} %get-tuple-element.19), custom_call_target="InvertDiagBlocksLowerTriangular" | custom-call | tf_op jit(solution)/shard_map/triangular_solve/custom-call.0 | solution.py:20
  227.6 0.6 fusion.8
  228.8 0.6 fusion.17
  229.4 1.0 fusion
  230.6 67.0 %all-reduce.10.cloned.1.call-done = f32[1024,256]{0,1:T(8,128)} async-done(((f32[1024,256]{0,1:T(8,128)}), f32[1024,256]{0,1:T(8,128)}) %all-reduce.10.cloned.1.call-update) | async-done | bytes 1048592 | tf_op jit(solution)/shard_map/psum | solution.py:11
  297.5 7.3 fusion.24
  304.9 146.3 %all-reduce.12.cloned.1.call-done = f32[256,1024]{1,0:T(8,128)} async-done(((f32[256,1024]{1,0:T(8,128)}), f32[256,1024]{1,0:T(8,128)}) %all-reduce.12.cloned.1.call-update) | async-done | bytes 1048592 | tf_op jit(solution)/shard_map/psum | solution.py:39
  451.2 7.2 convolution_subtract_fusion.1
  458.4 2.0 copy-done
  460.4 1.7 fusion.2
  462.4 1.3 slice_bitcast_fusion
  463.7 140.3 %all-reduce.14.cloned.1.call-done = f32[256,256]{0,1:T(8,128)} async-done(((f32[256,256]{0,1:T(8,128)}), f32[256,256]{0,1:T(8,128)}) %all-reduce.14.cloned.1.call-update) | async-done | bytes 262160 | tf_op jit(solution)/shard_map/psum | solution.py:25
  604.0 1.1 copy.8
  605.1 1.0 fusion.10
  606.1 11.7 %cholesky.164 = f32[128,128]{1,0:T(8,128)S(1)} custom-call(f32[128,128]{1,0:T(8,128)S(1)} %cholesky.197), custom_call_target="Cholesky" | custom-call | tf_op jit(solution)/shard_map/jit(cholesky)/cholesky | solution.py:19
  617.9 0.6 compare_reduce_fusion.1
  618.5 9.8 %custom-call.15 = f32[1,128,128]{1,2,0:T(8,128)S(1)} custom-call(f32[1,128,128]{2,1,0:T(8,128)S(1)} %get-tuple-element.47), custom_call_target="InvertDiagBlocksLowerTriangular" | custom-call | tf_op jit(solution)/shard_map/jit(cholesky)/cholesky | solution.py:19
  628.8 11.7 %cholesky.181 = f32[128,128]{1,0:T(8,128)S(1)} custom-call(f32[128,128]{1,0:T(8,128)S(1)} %convolution_subtract_fusion.4), custom_call_target="Cholesky" | custom-call | tf_op jit(solution)/shard_map/jit(cholesky)/cholesky | solution.py:19
  640.6 0.7 compare_reduce_fusion
  642.7 4.3 while.5
  643.5 1.4 bitcast_dynamic-update-slice_fusion.5
  645.6 1.4 bitcast_dynamic-update-slice_fusion.5
  647.0 19.7 %custom-call.16 = f32[2,128,128]{1,2,0:T(8,128)S(1)} custom-call(f32[2,128,128]{2,1,0:T(8,128)S(1)} %get-tuple-element.20), custom_call_target="InvertDiagBlocksLowerTriangular" | custom-call | tf_op jit(solution)/shard_map/triangular_solve/custom-call.0 | solution.py:20
  666.7 0.6 fusion.6
  667.9 0.6 fusion.13
  668.6 1.0 fusion.1
  669.7 66.9 %all-reduce.16.cloned.1.call-done = f32[1024,256]{0,1:T(8,128)} async-done(((f32[1024,256]{0,1:T(8,128)}), f32[1024,256]{0,1:T(8,128)}) %all-reduce.16.cloned.1.call-update) | async-done | bytes 1048592 | tf_op jit(solution)/shard_map/psum | solution.py:11
  736.6 7.3 fusion.25
  743.9 1.5 pad_maximum_fusion.1
  745.4 4.1 copy.10
  749.5 140.9 %all-reduce.18.cloned.1.call-done = f32[256,1024]{1,0:T(8,128)} async-done(((f32[256,1024]{1,0:T(8,128)}), f32[256,1024]{1,0:T(8,128)}) %all-reduce.18.cloned.1.call-update) | async-done | bytes 1048592 | tf_op jit(solution)/shard_map/psum | solution.py:39
  890.4 2.9 pad_maximum_fusion
  893.2 4.7 reshape.63
  897.9 6.7 convolution_subtract_fusion
  904.6 10.9 %copy.11 = f32[1024,4,1,256]{3,2,1,0:T(1,128)} copy(f32[1024,4,1,256]{0,3,1,2:T(8,128)} %bitcast.86) | data formatting | bytes 8388608
  (49 shorter events, 5.4 us)
Async XLA Ops:
  7.2 158.0 %all-reduce.8.cloned.1.call-start = ((), (), s32[]{:S(2)}) async-start(), calls=%async_computation | async-start | bytes 524288 | tf_op jit(solution)/shard_map/psum | solution.py:25
  21.5 276.0 %all-reduce.10.cloned.1.call-start = ((), (), s32[]{:S(2)}) async-start(), calls=%async_computation.1 | async-start | bytes 2097152 | tf_op jit(solution)/shard_map/psum | solution.py:11
  230.5 220.7 %all-reduce.12.cloned.1.call-start = ((), (), s32[]{:S(2)}) async-start(), calls=%async_computation.2 | async-start | bytes 2097152 | tf_op jit(solution)/shard_map/psum | solution.py:39
  297.5 153.7 %copy-start.1 = (f32[1024,256]{0,1:T(8,128)S(1)}, f32[1024,256]{0,1:T(8,128)}, u32[]{:S(2)}) copy-start(f32[1024,256]{0,1:T(8,128)} %all-reduce.10.cloned.1.call-done) | copy-start | bytes 3145732
  304.8 299.2 %all-reduce.14.cloned.1.call-start = ((), (), s32[]{:S(2)}) async-start(), calls=%async_computation.3 | async-start | bytes 524288 | tf_op jit(solution)/shard_map/psum | solution.py:25
  458.4 2.0 copy-start
  462.2 274.5 %all-reduce.16.cloned.1.call-start = ((), (), s32[]{:S(2)}) async-start(), calls=%async_computation.4 | async-start | bytes 2097152 | tf_op jit(solution)/shard_map/psum | solution.py:11
  669.6 220.7 %all-reduce.18.cloned.1.call-start = ((), (), s32[]{:S(2)}) async-start(), calls=%async_computation.5 | async-start | bytes 2097152 | tf_op jit(solution)/shard_map/psum | solution.py:39
  736.6 7.3 copy-start.2
  743.9 146.4 %copy-start.3 = (f32[256,1024]{1,0:T(8,128)S(1)}, f32[256,1024]{1,0:T(8,128)}, u32[]{:S(2)}) copy-start(f32[256,1024]{1,0:T(8,128)} %all-reduce.12.cloned.1.call-done) | copy-start | bytes 3145732
  890.4 7.6 copy-start.4
Sparse Core Ops, SparseCore 0:
  21.6 143.5 all-reduce.7
  230.6 66.8 all-reduce.9
  304.9 146.2 all-reduce.11
  462.3 141.6 all-reduce.13
  669.8 66.8 all-reduce.15
  744.0 146.2 all-reduce.17
where the time goes:
time: 936 us; the launch traced here: 923 us
  waiting for transfers between devices  704 us (75%)
  other arithmetic  116 us (12%)
  local copies, waits for them, and re-layouts  45.6 us (5%)
  matrix products  38.1 us (4%)
  between operations  17.3 us (2%)
    psum x2, waiting for transfers between devices, factor_project(): return (basis, lax.psum(product(basis.T, block), 'rows'))  287 us
    psum x2, waiting for transfers between devices, single_pass(): gram = lax.psum(product(panel.T, panel), 'rows')  283 us
    psum x2, waiting for transfers between devices, broadcast(): return lax.psum(jnp.where(mine, array, jnp.zeros_like(array)), axis)  134 us
    another operation x13, other arithmetic, lower_solve(): lower = jnp.linalg.cholesky(gram)  68.7 us
    another operation x5, other arithmetic, lower_solve(): lax.linalg.triangular_solve(lower, panel.T, left_side=True, lower=True)  39.4 us
    dot_general x6, matrix products, product(): return jnp.dot(left, right, precision=HIGHEST)  33.5 us
    unnamed x13, local copies, waits for them, and re-layouts  27.9 us
  transfers between devices with their start and end apart: 6, of which 6 were waited for; matrix products, arithmetic and copies ran while one was open for 1% of the time, Pallas kernels for 0%

commit v1 on v0

v1 whole, which is shorter than its diff:
```python
import jax
import jax.numpy as jnp
from jax import lax
from jax.experimental import pallas as pl
from jax.experimental.pallas import tpu as pltpu
from jax.sharding import PartitionSpec as P

HIGHEST = lax.Precision.HIGHEST
F32 = jnp.float32
BF16 = jnp.bfloat16
MESH = pl.DeviceIdType.MESH

NY = 4
NZ = 8
NX = 4
ROWS = 1024
WIDTH = 512
B = 128
GR = 8
TILES = 8
TY = 6
CH = 128
NCH = ROWS // CH


def dot(a, b, dims):
    return lax.dot_general(a, b, (dims, ((), ())), precision=HIGHEST, preferred_element_type=F32)


def split(value):
    high = value.astype(BF16)
    return high, (value - high.astype(F32)).astype(BF16)


def dot3(a, b, dims):
    def one(u, v):
        return lax.dot_general(u, v, (dims, ((), ())), preferred_element_type=F32)

    return one(a[0], b[0]) + (one(a[0], b[1]) + one(a[1], b[0]))

def rows_bcast(x, j):
    return jnp.broadcast_to(x[j:j + 1, :], x.shape)

def lane_bcast(x, c):
    return jnp.broadcast_to(x[:, c:c + 1], x.shape)

def leaf(x_ref):
    n = B // GR
    lane = lax.broadcasted_iota(jnp.int32, (GR, B), 1)
    sub = lax.broadcasted_iota(jnp.int32, (GR, B), 0)
    x = [x_ref[GR * t:GR * (t + 1), :] for t in range(n)]
    for g in range(n):
        base = GR * g
        cur = x[g]
        v = [lane_bcast(cur, base + c) for c in range(GR)]
        in_group = (lane >= base) & (lane < base + GR)
        scale, mult, rows = [], {}, []
        for j in range(GR):
            r = lax.rsqrt(rows_bcast(v[j], j))
            w = jnp.where(sub > j, v[j] * r, 0.0)
            row = jnp.where(lane == base + j, r, rows_bcast(cur, j) * r)
            cur = jnp.where(sub == j, row, jnp.where((lane == base + j) & (sub > j), 0.0, cur) - w * row)
            for c in range(j + 1, GR):
                m = rows_bcast(v[c], j) * r
                mult[j, c] = m
                v[c] = v[c] - w * m
            scale.append(r)
            rows.append(jnp.where(in_group & (lane > base + j), 0.0, row))
        x[g] = cur
        for t in range(g + 1, n):
            xt = x[t]
            u = [lane_bcast(xt, base + c) for c in range(GR)]
            xt = jnp.where(in_group, 0.0, xt)
            for j in range(GR):
                w = u[j] * scale[j]
                for c in range(j + 1, GR):
                    u[c] = u[c] - w * mult[j, c]
                xt = xt - w * rows[j]
            x[t] = xt
    for t in range(n):
        x_ref[GR * t:GR * (t + 1), :] = x[t]

def chol_inv(x_ref, d_ref):
    size = x_ref.shape[0]
    nb = size // B
    for k in range(nb):
        sl = slice(B * k, B * (k + 1))
        d_ref[...] = x_ref[sl, sl]
        leaf(d_ref)
        ri = lax.broadcasted_iota(jnp.int32, (B, B), 0)
        ci = lax.broadcasted_iota(jnp.int32, (B, B), 1)
        m = jnp.where(ri >= ci, d_ref[...], 0.0)
        x_ref[sl, sl] = m
        if k:
            left = dot(m, x_ref[sl, :B * k], ((1,), (0,)))
            x_ref[sl, :B * k] = left
        if k < nb - 1:
            hi = slice(B * (k + 1), size)
            up = dot(m, x_ref[sl, hi], ((1,), (0,)))
            x_ref[sl, hi] = jnp.zeros_like(up)
            lo = slice(B * (k + 1), size)
            x_ref[lo, hi] = x_ref[lo, hi] - dot(up, up, ((0,), (0,)))
            x_ref[lo, sl] = -dot(up, m, ((0,), (0,)))
            if k:
                x_ref[lo, :B * k] = x_ref[lo, :B * k] - dot(up, left, ((0,), (0,)))


def each(count, body):
    def step(i, carry):
        body(i + 1)
        return carry

    lax.fori_loop(0, count, step, 0)


def exchange(count, make):
    each(count, lambda d: make(d).start())


def arrived(count, make):
    each(count, lambda d: make(d).wait_recv())


def sent(count, make):
    each(count, lambda d: make(d).wait_send())


def gather_kernel(
    a_hbm, p_hbm, gram_hbm, g_hbm,
    av, pt, gs, gy, gsum, gz, gram, gl, gf, ry, sy, rz2, rz1, sz, ry2,
    load_sem, ring_s, ring_r, core_s, core_r, gy_s, gy_r, gz_s, gz_r, ga_s, ga_r, gx_s, gx_r, gc_s, gc_r,
    y1_s, y1_r, z1_s, z1_r, z2_s, z2_r, y2_s, y2_r, z3_s, z3_r, y3_s, y3_r, y4_s, y4_r, z4_s, z4_r, out_sem,
):
    row = lax.axis_index("rows")
    col = lax.axis_index("cols")
    y, z = row % NY, row // NY
    x, core = col // 2, col % 2

    def at_y(d):
        return (z * NY + (y + d) % NY, col)

    def at_z(d):
        return (((z + d) % NZ) * NY + y, col)

    def at_x(d):
        return (row, ((x + d) % NX) * 2 + core)

    other = (row, x * 2 + 1 - core)

    def remote(src, dst, send, recv, device):
        return pltpu.make_async_remote_copy(
            src_ref=src, dst_ref=dst, send_sem=send, recv_sem=recv, device_id=device, device_id_type=MESH
        )

    load = pltpu.make_async_copy(a_hbm, av, load_sem)
    load.start()

    barrier = pltpu.get_barrier_semaphore()

    def greet(device):
        pl.semaphore_signal(barrier, inc=1, device_id=device, device_id_type=MESH)

    each(NY - 1, lambda d: greet(at_y(d)))
    each(NZ - 1, lambda d: greet(at_z(d)))
    each(NX - 1, lambda d: greet(at_x(d)))
    greet(other)
    load.wait()
    pl.semaphore_wait(barrier, (NY - 1) + (NZ - 1) + (NX - 1) + 1)

    def chunk(i):
        return pt.at[pl.ds(2 * core, 2), pl.ds(pl.multiple_of(i * CH, CH), CH), :]

    def ring(i, d):
        return remote(chunk(i), chunk(i), ring_s.at[i], ring_r.at[i], at_x(d))

    def across(i):
        return remote(chunk(i), chunk(i), core_s.at[i], core_r.at[i], other)

    half = NCH // 2

    def loop(count, body):
        def step(i, carry):
            body(i)
            return carry

        lax.fori_loop(0, count, step, 0)

    @pl.when(x == 0)
    def _():
        for h in range(2):
            pt[2 * core + h] = av[pl.ds(h, ROWS, stride=TILES), :]

        def send(i):
            ring(i, 1).start()
            ring(half + i, NX - 1).start()
            across(i).start()
            across(half + i).start()

        loop(half, send)

    @pl.when(x == 1)
    def _():
        def first(i):
            ring(i, 1).wait_recv()
            ring(i, 1).start()
            across(i).start()

        def second(i):
            ring(half + i, 1).wait_recv()
            across(half + i).start()

        loop(half, first)
        loop(half, second)

    @pl.when(x == 2)
    def _():
        def both(i):
            ring(i, 1).wait_recv()
            ring(i, 1).start()
            across(i).start()
            ring(half + i, 1).wait_recv()
            ring(half + i, NX - 1).start()
            across(half + i).start()

        loop(half, both)

    @pl.when(x == 3)
    def _():
        def first(i):
            ring(half + i, 1).wait_recv()
            ring(half + i, NX - 1).start()
            across(half + i).start()

        def second(i):
            ring(i, 1).wait_recv()
            across(i).start()

        loop(half, first)
        loop(half, second)

    loop(NCH, lambda i: across(i).wait_recv())

    left = pt[x]
    for h in range(2):
        gs[h] = dot(left, pt[2 * core + h], ((0,), (0,)))

    def gram_y(d):
        return remote(gs, gy.at[y], gy_s.at[d - 1], gy_r.at[d - 1], at_y(d))

    exchange(NY - 1, gram_y)
    gy[y] = gs[...]

    panels = [split(jnp.concatenate([pt[q] for q in range(4)], axis=1))]

    def local_products(first, last):
        for t in range(first, last):
            gl[t] = dot3(panels[0], split(av[pl.ds(t, ROWS, stride=TILES), :]), ((0,), (0,)))

    local_products(0, 2)
    arrived(NY - 1, gram_y)
    gsum[...] = (gy[0] + gy[1]) + (gy[2] + gy[3])

    def rows16(ref, index):
        return ref.at[:, pl.ds(pl.multiple_of(index * 16, 16), 16), :]

    def gram_z(d):
        return remote(rows16(gsum, (z + d) % NZ), gz.at[z], gz_s.at[d - 1], gz_r.at[d - 1], at_z(d))

    exchange(NZ - 1, gram_z)
    gz[z] = gsum[:, pl.ds(pl.multiple_of(z * 16, 16), 16), :]
    local_products(2, 4)
    arrived(NZ - 1, gram_z)

    def gram_piece():
        return gram.at[x, pl.ds(2 * core, 2), pl.ds(pl.multiple_of(z * 16, 16), 16), :]

    total = gz[0]
    for i in range(1, NZ):
        total = total + gz[i]
    gram[x, pl.ds(2 * core, 2), pl.ds(pl.multiple_of(z * 16, 16), 16), :] = total

    def gram_all(d):
        return remote(gram_piece(), gram_piece(), ga_s.at[d - 1], ga_r.at[d - 1], at_z(d))

    exchange(NZ - 1, gram_all)
    local_products(4, 6)
    arrived(NZ - 1, gram_all)

    def gram_block(index):
        return gram.at[index, pl.ds(2 * core, 2), :, :]

    def gram_x(d):
        return remote(gram_block(x), gram_block(x), gx_s.at[d - 1], gx_r.at[d - 1], at_x(d))

    def gram_core(d):
        index = (x + NX - d) % NX
        return remote(gram_block(index), gram_block(index), gc_s.at[d], gc_r.at[d], other)

    exchange(NX - 1, gram_x)
    gram_core(0).start()
    local_products(6, 8)

    def rows_of(ref, lo, hi, index, size):
        return ref.at[lo:hi, pl.ds(pl.multiple_of(index * size, size), size), :]

    def y1(d):
        return remote(rows_of(gl, 0, TY, (y + d) % NY, 128), ry.at[d - 1], y1_s.at[d - 1], y1_r.at[d - 1], at_y(d))

    def z1(d):
        return remote(rows_of(gl, TY, TILES, (z + d) % NZ, 64), rz1.at[d - 1], z1_s.at[d - 1], z1_r.at[d - 1], at_z(d))

    exchange(NY - 1, y1)
    exchange(NZ - 1, z1)

    def pass_on(d):
        gram_x(d).wait_recv()
        gram_core(d).start()

    each(NX - 1, pass_on)

    arrived(NY - 1, y1)
    sy[...] = (gl[0:TY, pl.ds(pl.multiple_of(y * 128, 128), 128), :] + ry[0]) + (ry[1] + ry[2])

    def z2(d):
        return remote(rows_of(sy, 0, TY, (z + d) % NZ, 16), rz2.at[d - 1], z2_s.at[d - 1], z2_r.at[d - 1], at_z(d))

    exchange(NZ - 1, z2)
    arrived(NZ - 1, z1)
    total = gl[TY:TILES, pl.ds(pl.multiple_of(z * 64, 64), 64), :]
    for i in range(NZ - 1):
        total = total + rz1[i]
    sz[...] = total

    def y2(d):
        return remote(rows_of(sz, 0, TILES - TY, (y + d) % NY, 16), ry2.at[d - 1], y2_s.at[d - 1], y2_r.at[d - 1], at_y(d))

    exchange(NY - 1, y2)
    arrived(NZ - 1, z2)
    total = sy[:, pl.ds(pl.multiple_of(z * 16, 16), 16), :]
    for i in range(NZ - 1):
        total = total + rz2[i]
    gf[0:TY, pl.ds(pl.multiple_of((y * NZ + z) * 16, 16), 16), :] = total

    def z3(d):
        piece = rows_of(gf, 0, TY, y * NZ + z, 16)
        return remote(piece, piece, z3_s.at[d - 1], z3_r.at[d - 1], at_z(d))

    exchange(NZ - 1, z3)
    arrived(NY - 1, y2)
    total = sz[:, pl.ds(pl.multiple_of(y * 16, 16), 16), :]
    for i in range(NY - 1):
        total = total + ry2[i]
    gf[TY:TILES, pl.ds(pl.multiple_of((z * NY + y) * 16, 16), 16), :] = total

    def y3(d):
        piece = rows_of(gf, TY, TILES, z * NY + y, 16)
        return remote(piece, piece, y3_s.at[d - 1], y3_r.at[d - 1], at_y(d))

    exchange(NY - 1, y3)
    arrived(NZ - 1, z3)

    def y4(d):
        piece = rows_of(gf, 0, TY, y, 128)
        return remote(piece, piece, y4_s.at[d - 1], y4_r.at[d - 1], at_y(d))

    exchange(NY - 1, y4)
    arrived(NY - 1, y3)

    def z4(d):
        piece = rows_of(gf, TY, TILES, z, 64)
        return remote(piece, piece, z4_s.at[d - 1], z4_r.at[d - 1], at_z(d))

    exchange(NZ - 1, z4)
    for d in range(NX):
        gram_core(d).wait_recv()
    arrived(NY - 1, y4)
    arrived(NZ - 1, z4)

    outs = [
        pltpu.make_async_copy(src, dst, out_sem.at[i])
        for i, (src, dst) in enumerate([(pt, p_hbm), (gram, gram_hbm), (gf, g_hbm)])
    ]
    for copy in outs:
        copy.start()

    @pl.when(x == 0)
    def _():
        loop(half, lambda i: ring(i, 1).wait_send())
        loop(half, lambda i: ring(half + i, 1).wait_send())

    @pl.when(x == 1)
    def _():
        loop(half, lambda i: ring(i, 1).wait_send())

    @pl.when(x == 2)
    def _():
        loop(half, lambda i: ring(i, 1).wait_send())
        loop(half, lambda i: ring(half + i, 1).wait_send())

    @pl.when(x == 3)
    def _():
        loop(half, lambda i: ring(half + i, 1).wait_send())

    loop(NCH, lambda i: across(i).wait_send())
    for count, make in (
        (NY - 1, gram_y), (NZ - 1, gram_z), (NZ - 1, gram_all), (NX - 1, gram_x),
        (NY - 1, y1), (NZ - 1, z1), (NZ - 1, z2), (NY - 1, y2), (NZ - 1, z3), (NY - 1, y3), (NY - 1, y4), (NZ - 1, z4),
    ):
        sent(count, make)
    for d in range(NX):
        gram_core(d).wait_send()
    for copy in outs:
        copy.wait()


def gather_products(flat):
    dma = pltpu.SemaphoreType.DMA
    tz = TILES - TY
    y_pair = [dma((NY - 1,)), dma((NY - 1,))]
    z_pair = [dma((NZ - 1,)), dma((NZ - 1,))]
    x_pair = [dma((NX - 1,)), dma((NX - 1,))]
    any_space = pl.BlockSpec(memory_space=pl.ANY)
    return pl.pallas_call(
        gather_kernel,
        out_shape=(
            jax.ShapeDtypeStruct((4, ROWS, B), F32),
            jax.ShapeDtypeStruct((4, 4, B, B), F32),
            jax.ShapeDtypeStruct((TILES, WIDTH, B), F32),
        ),
        in_specs=[any_space],
        out_specs=(any_space,) * 3,
        scratch_shapes=[
            pltpu.VMEM((ROWS * TILES, B), F32),
            pltpu.VMEM((4, ROWS, B), F32),
            pltpu.VMEM((2, B, B), F32),
            pltpu.VMEM((NY, 2, B, B), F32),
            pltpu.VMEM((2, B, B), F32),
            pltpu.VMEM((NZ, 2, 16, B), F32),
            pltpu.VMEM((4, 4, B, B), F32),
            pltpu.VMEM((TILES, WIDTH, B), F32),
            pltpu.VMEM((TILES, WIDTH, B), F32),
            pltpu.VMEM((NY - 1, TY, 128, B), F32),
            pltpu.VMEM((TY, 128, B), F32),
            pltpu.VMEM((NZ - 1, TY, 16, B), F32),
            pltpu.VMEM((NZ - 1, tz, 64, B), F32),
            pltpu.VMEM((tz, 64, B), F32),
            pltpu.VMEM((NY - 1, tz, 16, B), F32),
            dma,
            dma((NCH,)), dma((NCH,)), dma((NCH,)), dma((NCH,)),
            *y_pair, *z_pair, *z_pair, *x_pair, dma((NX,)), dma((NX,)),
            *y_pair, *z_pair, *z_pair, *y_pair, *z_pair, *y_pair, *y_pair, *z_pair,
            dma((3,)),
        ],
        compiler_params=pltpu.CompilerParams(
            collective_id=0, has_side_effects=True, vmem_limit_bytes=48 << 20
        ),
        name="gather_products",
    )(flat)


def factor_kernel(gram_ref, m_ref, d_ref):
    for k in range(WIDTH // B):
        for t in range(WIDTH // B):
            block = gram_ref[k, t] if t >= k else jnp.zeros((B, B), F32)
            m_ref[B * k : B * (k + 1), B * t : B * (t + 1)] = block
    chol_inv(m_ref, d_ref)


def factor(gram):
    return pl.pallas_call(
        factor_kernel,
        out_shape=jax.ShapeDtypeStruct((WIDTH, WIDTH), F32),
        scratch_shapes=[pltpu.VMEM((B, B), F32)],
        compiler_params=pltpu.CompilerParams(vmem_limit_bytes=32 << 20),
        name="factor",
    )(gram)


def project_kernel(a_ref, p_ref, m_ref, g_ref, rows_ref, basis_ref, trail_ref, wh, wl):
    rows = p_ref.shape[1]
    inverse = split(m_ref[...])

    @pl.when(pl.program_id(0) == 0)
    def _():
        for t in range(TILES):
            w = dot3(inverse, split(g_ref[t]), ((1,), (0,)))
            rows_ref[pl.ds(t, WIDTH, stride=TILES), :] = w
            wh[t], wl[t] = split(w)

    panel = split(jnp.concatenate([p_ref[q] for q in range(4)], axis=1))
    basis = dot3(panel, inverse, ((1,), (1,)))
    for q in range(4):
        basis_ref[pl.ds((q % 2) * 2 + q // 2, rows, stride=4), :] = basis[:, B * q : B * (q + 1)]
    pair = split(basis)
    for t in range(TILES):
        spot = pl.ds(t, rows, stride=TILES)
        trail_ref[spot, :] = a_ref[spot, :] - dot3(pair, (wh[t], wl[t]), ((1,), (0,)))


def project(flat, panels, inverse, products):
    steps = 4
    rows = ROWS // steps
    return pl.pallas_call(
        project_kernel,
        grid=(steps,),
        out_shape=(
            jax.ShapeDtypeStruct((WIDTH * TILES, B), F32),
            jax.ShapeDtypeStruct((ROWS * 4, B), F32),
            jax.ShapeDtypeStruct((ROWS * TILES, B), F32),
        ),
        in_specs=[
            pl.BlockSpec((rows * TILES, B), lambda i: (i, 0)),
            pl.BlockSpec((4, rows, B), lambda i: (0, i, 0)),
            pl.BlockSpec((WIDTH, WIDTH), lambda i: (0, 0)),
            pl.BlockSpec((TILES, WIDTH, B), lambda i: (0, 0, 0)),
        ],
        out_specs=(
            pl.BlockSpec((WIDTH * TILES, B), lambda i: (0, 0)),
            pl.BlockSpec((rows * 4, B), lambda i: (i, 0)),
            pl.BlockSpec((rows * TILES, B), lambda i: (i, 0)),
        ),
        scratch_shapes=[pltpu.VMEM((TILES, WIDTH, B), BF16)] * 2,
        compiler_params=pltpu.CompilerParams(vmem_limit_bytes=40 << 20),
        name="project",
    )(flat, panels, inverse, products)


def on_device(features):
    flat = features.reshape(ROWS * TILES, B)
    panels, gram, products = gather_products(flat)
    inverse = factor(gram)
    factor_rows, basis, trailing = project(flat, panels, inverse, products)
    basis = basis.reshape(ROWS, 2, 2, B).transpose(0, 2, 1, 3).reshape(ROWS, 2, 256)
    return (factor_rows.reshape(WIDTH, 4, 1, 256), basis, trailing.reshape(features.shape))


def solution(mesh):
    placed = (P("rows", None, "cols", None),)
    return jax.shard_map(
        on_device,
        mesh=mesh,
        in_specs=placed,
        out_specs=(
            P(None, None, "cols", None),
            P("rows", None, None),
            P("rows", None, "cols", None),
        ),
        check_vma=False,
    )
```

time: 936 us -> 149 us (0.16)
  the two profiles are of different devices: /device:TPU:1 before, /device:TPU:18 now
where the time goes in v1:
time: 149 us
  Pallas kernels  148 us (99%)
    pallas_call x1, Pallas kernels, gather_products(): pl.pallas_call(gather_kernel, out_shape=(jax.ShapeDtypeStruct((4, ROWS, B...  114 us
    pallas_call x1, Pallas kernels, factor(): pl.pallas_call(factor_kernel, out_shape=jax.ShapeDtypeStruct((WIDTH, WIDT...  19.3 us
    pallas_call x1, Pallas kernels, project(): pl.pallas_call(project_kernel, grid=(steps,), out_shape=(jax.ShapeDtypeSt...  14.9 us

profile of v1, /device:TPU:18, one launch (start us, length us, event | category | flops | bytes accessed | tf_op | source)
XLA Modules:
  0.0 148.5 jit_solution(865109685481032588)
XLA Ops:
  0.6 0.0 copy-start
  0.6 113.6 %gather_products.1 = (f32[4,1024,128]{2,1,0:T(8,128)S(1)}, f32[4,4,128,128]{3,2,1,0:T(8,128)S(1)}, f32[8,512,128]{2,1,0:T(8,128)S(1)}) custom-call(f32[8192,128]{1,0:T(8,128)} %bitcast.8), custom_call_target="tpu_custom_call" | custom-call | tf_op jit(solution)/shard_map/gather_products/pallas_call | solution.py:423
  114.3 19.3 %factor.1.m_ref = f32[512,512]{1,0:T(8,128)S(1)} custom-call(f32[4,4,128,128]{3,2,1,0:T(8,128)S(1)} %get-tuple-element.10.gram_ref), custom_call_target="tpu_custom_call" | custom-call | tf_op jit(solution)/shard_map/factor/pallas_call | solution.py:470
  133.6 0.0 copy-done
  133.6 14.9 %project.1 = (f32[4096,128]{1,0:T(8,128)}, f32[4096,128]{1,0:T(8,128)}, f32[8192,128]{1,0:T(8,128)}) custom-call(f32[8192,128]{1,0:T(8,128)S(1)} %bitcast.9, f32[4,1024,128]{2,1,0:T(8,128)S(1)} %get-tuple-element.9.p_ref, f32[512,512]{1,0:T(8,128)S(1)} %factor.1.m_ref, f32[8,512,128]{2,1,0:T(8,128)S(1)} %get-tuple-element.11.g_ref), custom_call_target="tpu_custom_call" | custom-call | tf_op jit(solution)/shard_map/project/pallas_call | solution.py:503
Async XLA Ops:
  0.6 133.0 %copy-start = (f32[1024,4,1,256]{3,2,1,0:T(1,128)S(1)}, f32[1024,4,1,256]{3,2,1,0:T(1,128)}, u32[]{:S(2)}) copy-start(f32[1024,4,1,256]{3,2,1,0:T(1,128)} %param.1) | copy-start | bytes 12582916

commit v2 on v1

--- a/solution.py
+++ b/solution.py
@@ -19,7 +19,7 @@
 GR = 8
 TILES = 8
 TY = 6
-CH = 128
+CH = 64
 NCH = ROWS // CH
 
 
@@ -80,29 +80,26 @@
     for t in range(n):
         x_ref[GR * t:GR * (t + 1), :] = x[t]
 
-def chol_inv(x_ref, d_ref):
-    size = x_ref.shape[0]
-    nb = size // B
-    for k in range(nb):
-        sl = slice(B * k, B * (k + 1))
-        d_ref[...] = x_ref[sl, sl]
-        leaf(d_ref)
-        ri = lax.broadcasted_iota(jnp.int32, (B, B), 0)
-        ci = lax.broadcasted_iota(jnp.int32, (B, B), 1)
-        m = jnp.where(ri >= ci, d_ref[...], 0.0)
-        x_ref[sl, sl] = m
+def factor_step(k, m_ref, d_ref):
+    size = m_ref.shape[0]
+    sl = slice(B * k, B * (k + 1))
+    d_ref[...] = m_ref[sl, sl]
+    leaf(d_ref)
+    ri = lax.broadcasted_iota(jnp.int32, (B, B), 0)
+    ci = lax.broadcasted_iota(jnp.int32, (B, B), 1)
+    m = jnp.where(ri >= ci, d_ref[...], 0.0)
+    m_ref[sl, sl] = m
+    if k:
+        left = dot(m, m_ref[sl, : B * k], ((1,), (0,)))
+        m_ref[sl, : B * k] = left
+    if B * (k + 1) < size:
+        rest = slice(B * (k + 1), size)
+        up = dot(m, m_ref[sl, rest], ((1,), (0,)))
+        m_ref[sl, rest] = jnp.zeros_like(up)
+        m_ref[rest, rest] = m_ref[rest, rest] - dot(up, up, ((0,), (0,)))
+        m_ref[rest, sl] = -dot(up, m, ((0,), (0,)))
         if k:
-            left = dot(m, x_ref[sl, :B * k], ((1,), (0,)))
-            x_ref[sl, :B * k] = left
-        if k < nb - 1:
-            hi = slice(B * (k + 1), size)
-            up = dot(m, x_ref[sl, hi], ((1,), (0,)))
-            x_ref[sl, hi] = jnp.zeros_like(up)
-            lo = slice(B * (k + 1), size)
-            x_ref[lo, hi] = x_ref[lo, hi] - dot(up, up, ((0,), (0,)))
-            x_ref[lo, sl] = -dot(up, m, ((0,), (0,)))
-            if k:
-                x_ref[lo, :B * k] = x_ref[lo, :B * k] - dot(up, left, ((0,), (0,)))
+            m_ref[rest, : B * k] = m_ref[rest, : B * k] - dot(up, left, ((0,), (0,)))
 
 
 def each(count, body):
@@ -126,8 +123,8 @@
 
 
 def gather_kernel(
-    a_hbm, p_hbm, gram_hbm, g_hbm,
-    av, pt, gs, gy, gsum, gz, gram, gl, gf, ry, sy, rz2, rz1, sz, ry2,
+    a_hbm, p_hbm, m_hbm, g_hbm,
+    av, pt, ph, pl_, mm, dd, gs, gy, gsum, gz, gram, gl, gf, ry, sy, rz2, rz1, sz, ry2,
     load_sem, ring_s, ring_r, core_s, core_r, gy_s, gy_r, gz_s, gz_r, ga_s, ga_r, gx_s, gx_r, gc_s, gc_r,
     y1_s, y1_r, z1_s, z1_r, z2_s, z2_r, y2_s, y2_r, z3_s, z3_r, y3_s, y3_r, y4_s, y4_r, z4_s, z4_r, out_sem,
 ):
@@ -152,8 +149,14 @@
             src_ref=src, dst_ref=dst, send_sem=send, recv_sem=recv, device_id=device, device_id_type=MESH
         )
 
-    load = pltpu.make_async_copy(a_hbm, av, load_sem)
-    load.start()
+    def load(i):
+        part = pl.ds(i * CH * TILES, CH * TILES)
+        return pltpu.make_async_copy(a_hbm.at[part, :], av.at[part, :], load_sem.at[i])
+
+    half = NCH // 2
+    for i in range(half):
+        load(i).start()
+        load(half + i).start()
 
     barrier = pltpu.get_barrier_semaphore()
 
@@ -164,7 +167,6 @@
     each(NZ - 1, lambda d: greet(at_z(d)))
     each(NX - 1, lambda d: greet(at_x(d)))
     greet(other)
-    load.wait()
     pl.semaphore_wait(barrier, (NY - 1) + (NZ - 1) + (NX - 1) + 1)
 
     def chunk(i):
@@ -175,8 +177,6 @@
 
     def across(i):
         return remote(chunk(i), chunk(i), core_s.at[i], core_r.at[i], other)
-
-    half = NCH // 2
 
     def loop(count, body):
         def step(i, carry):
@@ -187,16 +187,20 @@
 
     @pl.when(x == 0)
     def _():
-        for h in range(2):
-            pt[2 * core + h] = av[pl.ds(h, ROWS, stride=TILES), :]
-
-        def send(i):
+        for i in range(half):
+            for j in (i, half + i):
+                load(j).wait()
+                for h in range(2):
+                    pt[2 * core + h, CH * j : CH * (j + 1), :] = av[pl.ds(CH * TILES * j + h, CH, stride=TILES), :]
             ring(i, 1).start()
             ring(half + i, NX - 1).start()
             across(i).start()
             across(half + i).start()
 
-        loop(half, send)
+    @pl.when(x > 0)
+    def _():
+        for i in range(NCH):
+            load(i).wait()
 
     @pl.when(x == 1)
     def _():
@@ -250,13 +254,36 @@
     exchange(NY - 1, gram_y)
     gy[y] = gs[...]
 
-    panels = [split(jnp.concatenate([pt[q] for q in range(4)], axis=1))]
-
-    def local_products(first, last):
-        for t in range(first, last):
-            gl[t] = dot3(panels[0], split(av[pl.ds(t, ROWS, stride=TILES), :]), ((0,), (0,)))
-
-    local_products(0, 2)
+    for q in range(4):
+        high, low = split(pt[q])
+        ph[B * q : B * (q + 1), :] = high.T
+        pl_[B * q : B * (q + 1), :] = low.T
+
+    def local_products(t):
+        tiles = [av[pl.ds(t + h, ROWS, stride=TILES), :] for h in range(2)]
+        out = dot3((ph[...], pl_[...]), split(jnp.concatenate(tiles, axis=1)), ((1,), (0,)))
+        gl[t] = out[:, :B]
+        gl[t + 1] = out[:, B:]
+
+    def rows_of(ref, lo, hi, index, size):
+        return ref.at[lo:hi, pl.ds(pl.multiple_of(index * size, size), size), :]
+
+    def y1(pair):
+        lo = 2 * pair
+
+        def make(d):
+            src = rows_of(gl, lo, lo + 2, (y + d) % NY, 128)
+            return remote(src, ry.at[d - 1, lo : lo + 2], y1_s.at[pair, d - 1], y1_r.at[pair, d - 1], at_y(d))
+
+        return make
+
+    def z1(d):
+        return remote(rows_of(gl, TY, TILES, (z + d) % NZ, 64), rz1.at[d - 1], z1_s.at[d - 1], z1_r.at[d - 1], at_z(d))
+
+    local_products(0)
+    exchange(NY - 1, y1(0))
+    local_products(6)
+    exchange(NZ - 1, z1)
     arrived(NY - 1, gram_y)
     gsum[...] = (gy[0] + gy[1]) + (gy[2] + gy[3])
 
@@ -268,7 +295,8 @@
 
     exchange(NZ - 1, gram_z)
     gz[z] = gsum[:, pl.ds(pl.multiple_of(z * 16, 16), 16), :]
-    local_products(2, 4)
+    local_products(2)
+    exchange(NY - 1, y1(1))
     arrived(NZ - 1, gram_z)
 
     def gram_piece():
@@ -283,7 +311,8 @@
         return remote(gram_piece(), gram_piece(), ga_s.at[d - 1], ga_r.at[d - 1], at_z(d))
 
     exchange(NZ - 1, gram_all)
-    local_products(4, 6)
+    local_products(4)
+    exchange(NY - 1, y1(2))
     arrived(NZ - 1, gram_all)
 
     def gram_block(index):
@@ -298,19 +327,6 @@
 
     exchange(NX - 1, gram_x)
     gram_core(0).start()
-    local_products(6, 8)
-
-    def rows_of(ref, lo, hi, index, size):
-        return ref.at[lo:hi, pl.ds(pl.multiple_of(index * size, size), size), :]
-
-    def y1(d):
-        return remote(rows_of(gl, 0, TY, (y + d) % NY, 128), ry.at[d - 1], y1_s.at[d - 1], y1_r.at[d - 1], at_y(d))
-
-    def z1(d):
-        return remote(rows_of(gl, TY, TILES, (z + d) % NZ, 64), rz1.at[d - 1], z1_s.at[d - 1], z1_r.at[d - 1], at_z(d))
-
-    exchange(NY - 1, y1)
-    exchange(NZ - 1, z1)
 
     def pass_on(d):
         gram_x(d).wait_recv()
@@ -318,7 +334,8 @@
 
     each(NX - 1, pass_on)
 
-    arrived(NY - 1, y1)
+    for pair in range(TY // 2):
+        arrived(NY - 1, y1(pair))
     sy[...] = (gl[0:TY, pl.ds(pl.multiple_of(y * 128, 128), 128), :] + ry[0]) + (ry[1] + ry[2])
 
     def z2(d):
@@ -335,6 +352,14 @@
         return remote(rows_of(sz, 0, TILES - TY, (y + d) % NY, 16), ry2.at[d - 1], y2_s.at[d - 1], y2_r.at[d - 1], at_y(d))
 
     exchange(NY - 1, y2)
+
+    for d in range(NX):
+        gram_core(d).wait_recv()
+    for k in range(4):
+        for t in range(4):
+            mm[B * k : B * (k + 1), B * t : B * (t + 1)] = gram[k, t] if t >= k else jnp.zeros((B, B), F32)
+    factor_step(0, mm, dd)
+
     arrived(NZ - 1, z2)
     total = sy[:, pl.ds(pl.multiple_of(z * 16, 16), 16), :]
     for i in range(NZ - 1):
@@ -357,6 +382,7 @@
         return remote(piece, piece, y3_s.at[d - 1], y3_r.at[d - 1], at_y(d))
 
     exchange(NY - 1, y3)
+    factor_step(1, mm, dd)
     arrived(NZ - 1, z3)
 
     def y4(d):
@@ -371,14 +397,14 @@
         return remote(piece, piece, z4_s.at[d - 1], z4_r.at[d - 1], at_z(d))
 
     exchange(NZ - 1, z4)
-    for d in range(NX):
-        gram_core(d).wait_recv()
+    factor_step(2, mm, dd)
+    factor_step(3, mm, dd)
     arrived(NY - 1, y4)
     arrived(NZ - 1, z4)
 
     outs = [
         pltpu.make_async_copy(src, dst, out_sem.at[i])
-        for i, (src, dst) in enumerate([(pt, p_hbm), (gram, gram_hbm), (gf, g_hbm)])
+        for i, (src, dst) in enumerate([(pt, p_hbm), (mm, m_hbm), (gf, g_hbm)])
     ]
     for copy in outs:
         copy.start()
@@ -404,7 +430,7 @@
     loop(NCH, lambda i: across(i).wait_send())
     for count, make in (
         (NY - 1, gram_y), (NZ - 1, gram_z), (NZ - 1, gram_all), (NX - 1, gram_x),
-        (NY - 1, y1), (NZ - 1, z1), (NZ - 1, z2), (NY - 1, y2), (NZ - 1, z3), (NY - 1, y3), (NY - 1, y4), (NZ - 1, z4),
+        (NY - 1, y1(0)), (NY - 1, y1(1)), (NY - 1, y1(2)), (NZ - 1, z1), (NZ - 1, z2), (NY - 1, y2), (NZ - 1, z3), (NY - 1, y3), (NY - 1, y4), (NZ - 1, z4),
     ):
         sent(count, make)
     for d in range(NX):
@@ -424,7 +450,7 @@
         gather_kernel,
         out_shape=(
             jax.ShapeDtypeStruct((4, ROWS, B), F32),
-            jax.ShapeDtypeStruct((4, 4, B, B), F32),
+            jax.ShapeDtypeStruct((WIDTH, WIDTH), F32),
             jax.ShapeDtypeStruct((TILES, WIDTH, B), F32),
         ),
         in_specs=[any_space],
@@ -432,6 +458,10 @@
         scratch_shapes=[
             pltpu.VMEM((ROWS * TILES, B), F32),
             pltpu.VMEM((4, ROWS, B), F32),
+            pltpu.VMEM((WIDTH, ROWS), BF16),
+            pltpu.VMEM((WIDTH, ROWS), BF16),
+            pltpu.VMEM((WIDTH, WIDTH), F32),
+            pltpu.VMEM((B, B), F32),
             pltpu.VMEM((2, B, B), F32),
             pltpu.VMEM((NY, 2, B, B), F32),
             pltpu.VMEM((2, B, B), F32),
@@ -445,10 +475,10 @@
             pltpu.VMEM((NZ - 1, tz, 64, B), F32),
             pltpu.VMEM((tz, 64, B), F32),
             pltpu.VMEM((NY - 1, tz, 16, B), F32),
-            dma,
+            dma((NCH,)),
             dma((NCH,)), dma((NCH,)), dma((NCH,)), dma((NCH,)),
             *y_pair, *z_pair, *z_pair, *x_pair, dma((NX,)), dma((NX,)),
-            *y_pair, *z_pair, *z_pair, *y_pair, *z_pair, *y_pair, *y_pair, *z_pair,
+            dma((TY // 2, NY - 1)), dma((TY // 2, NY - 1)), *z_pair, *z_pair, *y_pair, *z_pair, *y_pair, *y_pair, *z_pair,
             dma((3,)),
         ],
         compiler_params=pltpu.CompilerParams(
@@ -458,43 +488,32 @@
     )(flat)
 
 
-def factor_kernel(gram_ref, m_ref, d_ref):
-    for k in range(WIDTH // B):
-        for t in range(WIDTH // B):
-            block = gram_ref[k, t] if t >= k else jnp.zeros((B, B), F32)
-            m_ref[B * k : B * (k + 1), B * t : B * (t + 1)] = block
-    chol_inv(m_ref, d_ref)
-
-
-def factor(gram):
-    return pl.pallas_call(
-        factor_kernel,
-        out_shape=jax.ShapeDtypeStruct((WIDTH, WIDTH), F32),
-        scratch_shapes=[pltpu.VMEM((B, B), F32)],
-        compiler_params=pltpu.CompilerParams(vmem_limit_bytes=32 << 20),
-        name="factor",
-    )(gram)
-
-
 def project_kernel(a_ref, p_ref, m_ref, g_ref, rows_ref, basis_ref, trail_ref, wh, wl):
     rows = p_ref.shape[1]
     inverse = split(m_ref[...])
+    half = WIDTH // 2
 
     @pl.when(pl.program_id(0) == 0)
     def _():
-        for t in range(TILES):
-            w = dot3(inverse, split(g_ref[t]), ((1,), (0,)))
-            rows_ref[pl.ds(t, WIDTH, stride=TILES), :] = w
-            wh[t], wl[t] = split(w)
+        for t in range(0, TILES, 2):
+            g = split(jnp.concatenate([g_ref[t], g_ref[t + 1]], axis=1))
+            upper = dot3([v[:half, :half] for v in inverse], [v[:half] for v in g], ((1,), (0,)))
+            lower = dot3([v[half:] for v in inverse], g, ((1,), (0,)))
+            w = jnp.concatenate([upper, lower], axis=0)
+            for h in range(2):
+                rows_ref[pl.ds(t + h, WIDTH, stride=TILES), :] = w[:, B * h : B * (h + 1)]
+            wh[t // 2], wl[t // 2] = split(w)
 
     panel = split(jnp.concatenate([p_ref[q] for q in range(4)], axis=1))
     basis = dot3(panel, inverse, ((1,), (1,)))
     for q in range(4):
         basis_ref[pl.ds((q % 2) * 2 + q // 2, rows, stride=4), :] = basis[:, B * q : B * (q + 1)]
     pair = split(basis)
-    for t in range(TILES):
-        spot = pl.ds(t, rows, stride=TILES)
-        trail_ref[spot, :] = a_ref[spot, :] - dot3(pair, (wh[t], wl[t]), ((1,), (0,)))
+    for t in range(0, TILES, 2):
+        part = dot3(pair, (wh[t // 2], wl[t // 2]), ((1,), (0,)))
+        for h in range(2):
+            spot = pl.ds(t + h, rows, stride=TILES)
+            trail_ref[spot, :] = a_ref[spot, :] - part[:, B * h : B * (h + 1)]
 
 
 def project(flat, panels, inverse, products):
@@ -519,7 +538,7 @@
             pl.BlockSpec((rows * 4, B), lambda i: (i, 0)),
             pl.BlockSpec((rows * TILES, B), lambda i: (i, 0)),
         ),
-        scratch_shapes=[pltpu.VMEM((TILES, WIDTH, B), BF16)] * 2,
+        scratch_shapes=[pltpu.VMEM((TILES // 2, WIDTH, 2 * B), BF16)] * 2,
         compiler_params=pltpu.CompilerParams(vmem_limit_bytes=40 << 20),
         name="project",
     )(flat, panels, inverse, products)
@@ -527,8 +546,7 @@
 
 def on_device(features):
     flat = features.reshape(ROWS * TILES, B)
-    panels, gram, products = gather_products(flat)
-    inverse = factor(gram)
+    panels, inverse, products = gather_products(flat)
     factor_rows, basis, trailing = project(flat, panels, inverse, products)
     basis = basis.reshape(ROWS, 2, 2, B).transpose(0, 2, 1, 3).reshape(ROWS, 2, 256)
     return (factor_rows.reshape(WIDTH, 4, 1, 256), basis, trailing.reshape(features.shape))

time: 149 us -> 120 us (0.81)
  the two profiles are of different devices: /device:TPU:18 before, /device:TPU:1 now
where the time goes in v2:
time: 120 us; the launch traced here: 118 us
  Pallas kernels  118 us (98%)
    pallas_call x1, Pallas kernels, gather_products(): pl.pallas_call(gather_kernel, out_shape=(jax.ShapeDtypeStruct((4, ROWS, B...  107 us
    pallas_call x1, Pallas kernels, project(): pl.pallas_call(project_kernel, grid=(steps,), out_shape=(jax.ShapeDtypeSt...  10.2 us

profile of v2, /device:TPU:1, one launch (start us, length us, event | category | flops | bytes accessed | tf_op | source)
XLA Modules:
  0.0 118.2 jit_solution(4179357154909702523)
XLA Ops:
  0.6 0.0 copy-start
  0.6 107.3 %gather_products.1 = (f32[4,1024,128]{2,1,0:T(8,128)S(1)}, f32[512,512]{1,0:T(8,128)S(1)}, f32[8,512,128]{2,1,0:T(8,128)S(1)}) custom-call(f32[8192,128]{1,0:T(8,128)} %bitcast.8), custom_call_target="tpu_custom_call" | custom-call | tf_op jit(solution)/shard_map/gather_products/pallas_call | solution.py:449
  107.9 0.0 copy-done
  107.9 10.2 %project.1 = (f32[4096,128]{1,0:T(8,128)}, f32[4096,128]{1,0:T(8,128)}, f32[8192,128]{1,0:T(8,128)}) custom-call(f32[8192,128]{1,0:T(8,128)S(1)} %bitcast.9, f32[4,1024,128]{2,1,0:T(8,128)S(1)} %get-tuple-element.9.p_ref, f32[512,512]{1,0:T(8,128)S(1)} %get-tuple-element.10.m_ref, f32[8,512,128]{2,1,0:T(8,128)S(1)} %get-tuple-element.11.g_ref), custom_call_target="tpu_custom_call" | custom-call | tf_op jit(solution)/shard_map/project/pallas_call | solution.py:522
Async XLA Ops:
  0.6 107.3 %copy-start = (f32[1024,4,1,256]{3,2,1,0:T(1,128)S(1)}, f32[1024,4,1,256]{3,2,1,0:T(1,128)}, u32[]{:S(2)}) copy-start(f32[1024,4,1,256]{3,2,1,0:T(1,128)} %param.1) | copy-start | bytes 12582916

commit v3 on v2

--- a/solution.py
+++ b/solution.py
@@ -18,7 +18,7 @@
 B = 128
 GR = 8
 TILES = 8
-TY = 6
+TY = 4
 CH = 64
 NCH = ROWS // CH
 
@@ -44,12 +44,14 @@
 def lane_bcast(x, c):
     return jnp.broadcast_to(x[:, c:c + 1], x.shape)
 
-def leaf(x_ref):
+def leaf(x_ref, hook):
     n = B // GR
     lane = lax.broadcasted_iota(jnp.int32, (GR, B), 1)
     sub = lax.broadcasted_iota(jnp.int32, (GR, B), 0)
     x = [x_ref[GR * t:GR * (t + 1), :] for t in range(n)]
     for g in range(n):
+        if hook is not None and g == n // 2:
+            hook()
         base = GR * g
         cur = x[g]
         v = [lane_bcast(cur, base + c) for c in range(GR)]
@@ -80,11 +82,11 @@
     for t in range(n):
         x_ref[GR * t:GR * (t + 1), :] = x[t]
 
-def factor_step(k, m_ref, d_ref):
+def factor_step(k, m_ref, d_ref, hook=None):
     size = m_ref.shape[0]
     sl = slice(B * k, B * (k + 1))
     d_ref[...] = m_ref[sl, sl]
-    leaf(d_ref)
+    leaf(d_ref, hook)
     ri = lax.broadcasted_iota(jnp.int32, (B, B), 0)
     ci = lax.broadcasted_iota(jnp.int32, (B, B), 1)
     m = jnp.where(ri >= ci, d_ref[...], 0.0)
@@ -124,9 +126,9 @@
 
 def gather_kernel(
     a_hbm, p_hbm, m_hbm, g_hbm,
-    av, pt, ph, pl_, mm, dd, gs, gy, gsum, gz, gram, gl, gf, ry, sy, rz2, rz1, sz, ry2,
+    av, pt, ph, pl_, mm, dd, gs, gy, gsum, gz, gram, gl, gf, ry, sy, rz2, first_in, in_r, in_l, out_r, out_l, sz, ry2,
     load_sem, ring_s, ring_r, core_s, core_r, gy_s, gy_r, gz_s, gz_r, ga_s, ga_r, gx_s, gx_r, gc_s, gc_r,
-    y1_s, y1_r, z1_s, z1_r, z2_s, z2_r, y2_s, y2_r, z3_s, z3_r, y3_s, y3_r, y4_s, y4_r, z4_s, z4_r, out_sem,
+    y1_s, y1_r, sum_s, sum_r, z2_s, z2_r, y2_s, y2_r, z3_s, z3_r, y3_s, y3_r, y4_s, y4_r, all_s, all_r, out_sem,
 ):
     row = lax.axis_index("rows")
     col = lax.axis_index("cols")
@@ -277,13 +279,44 @@
 
         return make
 
-    def z1(d):
-        return remote(rows_of(gl, TY, TILES, (z + d) % NZ, 64), rz1.at[d - 1], z1_s.at[d - 1], z1_r.at[d - 1], at_z(d))
-
+    ways = ((1, in_r, out_r), (NZ - 1, in_l, out_l))
+    near = TY + (TILES - TY) // 2
+
+    def block(lo, hi, index):
+        return gl[lo:hi, pl.ds(pl.multiple_of((index % NZ) * 64, 64), 64), :]
+
+    def z_sum(hop, way):
+        to, into, out = ways[way]
+        if hop == 0:
+            lo, hi = (TY, near) if way == 0 else (near, TILES)
+            src, dst = rows_of(gl, lo, hi, (z + 4) % NZ, 64), first_in.at[way]
+        else:
+            src, dst = out.at[hop - 1], into.at[hop - 1]
+        return remote(src, dst, sum_s.at[way, hop], sum_r.at[way, hop], at_z(to))
+
+    def z_hop(hop):
+        for way, (to, into, out) in enumerate(ways):
+            if hop > 0:
+                z_sum(hop - 1, way).wait_recv()
+                index = z + (4 - hop) if way == 0 else z + NZ - (4 - hop)
+                low, high = block(TY, near, index), block(near, TILES, index)
+                if hop == 1:
+                    low, high = (low + first_in[0], high) if way == 0 else (low, high + first_in[1])
+                else:
+                    cut = near - TY
+                    low, high = low + into[hop - 2, :cut], high + into[hop - 2, cut:]
+                out[hop - 1, : near - TY] = low
+                out[hop - 1, near - TY :] = high
+            z_sum(hop, way).start()
+
+    local_products(4)
+    local_products(6)
+    z_hop(0)
     local_products(0)
     exchange(NY - 1, y1(0))
-    local_products(6)
-    exchange(NZ - 1, z1)
+    z_hop(1)
+    local_products(2)
+    exchange(NY - 1, y1(1))
     arrived(NY - 1, gram_y)
     gsum[...] = (gy[0] + gy[1]) + (gy[2] + gy[3])
 
@@ -295,8 +328,7 @@
 
     exchange(NZ - 1, gram_z)
     gz[z] = gsum[:, pl.ds(pl.multiple_of(z * 16, 16), 16), :]
-    local_products(2)
-    exchange(NY - 1, y1(1))
+    z_hop(2)
     arrived(NZ - 1, gram_z)
 
     def gram_piece():
@@ -311,8 +343,7 @@
         return remote(gram_piece(), gram_piece(), ga_s.at[d - 1], ga_r.at[d - 1], at_z(d))
 
     exchange(NZ - 1, gram_all)
-    local_products(4)
-    exchange(NY - 1, y1(2))
+    z_hop(3)
     arrived(NZ - 1, gram_all)
 
     def gram_block(index):
@@ -332,8 +363,6 @@
         gram_x(d).wait_recv()
         gram_core(d).start()
 
-    each(NX - 1, pass_on)
-
     for pair in range(TY // 2):
         arrived(NY - 1, y1(pair))
     sy[...] = (gl[0:TY, pl.ds(pl.multiple_of(y * 128, 128), 128), :] + ry[0]) + (ry[1] + ry[2])
@@ -342,16 +371,15 @@
         return remote(rows_of(sy, 0, TY, (z + d) % NZ, 16), rz2.at[d - 1], z2_s.at[d - 1], z2_r.at[d - 1], at_z(d))
 
     exchange(NZ - 1, z2)
-    arrived(NZ - 1, z1)
-    total = gl[TY:TILES, pl.ds(pl.multiple_of(z * 64, 64), 64), :]
-    for i in range(NZ - 1):
-        total = total + rz1[i]
-    sz[...] = total
+    for way in range(2):
+        z_sum(3, way).wait_recv()
+    sz[...] = block(TY, TILES, z) + (in_r[2] + in_l[2])
 
     def y2(d):
         return remote(rows_of(sz, 0, TILES - TY, (y + d) % NY, 16), ry2.at[d - 1], y2_s.at[d - 1], y2_r.at[d - 1], at_y(d))
 
     exchange(NY - 1, y2)
+    each(NX - 1, pass_on)
 
     for d in range(NX):
         gram_core(d).wait_recv()
@@ -382,25 +410,40 @@
         return remote(piece, piece, y3_s.at[d - 1], y3_r.at[d - 1], at_y(d))
 
     exchange(NY - 1, y3)
-    factor_step(1, mm, dd)
-    arrived(NZ - 1, z3)
 
     def y4(d):
         piece = rows_of(gf, 0, TY, y, 128)
         return remote(piece, piece, y4_s.at[d - 1], y4_r.at[d - 1], at_y(d))
 
+    def z_all(hop, way):
+        to = ways[way][0]
+        index = (z + NZ - hop) % NZ if way == 0 else (z + hop) % NZ
+        lo, hi = TY, TILES
+        if hop == 3:
+            lo, hi = (TY, near) if way == 0 else (near, TILES)
+        piece = rows_of(gf, lo, hi, index, 64)
+        return remote(piece, piece, all_s.at[way, hop], all_r.at[way, hop], at_z(to))
+
+    def hop(number):
+        for way in range(2):
+            if number:
+                z_all(number - 1, way).wait_recv()
+            z_all(number, way).start()
+
+    def begin():
+        arrived(NY - 1, y3)
+        hop(0)
+
+    factor_step(1, mm, dd, begin)
+    arrived(NZ - 1, z3)
     exchange(NY - 1, y4)
-    arrived(NY - 1, y3)
-
-    def z4(d):
-        piece = rows_of(gf, TY, TILES, z, 64)
-        return remote(piece, piece, z4_s.at[d - 1], z4_r.at[d - 1], at_z(d))
-
-    exchange(NZ - 1, z4)
-    factor_step(2, mm, dd)
+    hop(1)
+    factor_step(2, mm, dd, lambda: hop(2))
+    hop(3)
     factor_step(3, mm, dd)
     arrived(NY - 1, y4)
-    arrived(NZ - 1, z4)
+    for way in range(2):
+        z_all(3, way).wait_recv()
 
     outs = [
         pltpu.make_async_copy(src, dst, out_sem.at[i])
@@ -430,11 +473,15 @@
     loop(NCH, lambda i: across(i).wait_send())
     for count, make in (
         (NY - 1, gram_y), (NZ - 1, gram_z), (NZ - 1, gram_all), (NX - 1, gram_x),
-        (NY - 1, y1(0)), (NY - 1, y1(1)), (NY - 1, y1(2)), (NZ - 1, z1), (NZ - 1, z2), (NY - 1, y2), (NZ - 1, z3), (NY - 1, y3), (NY - 1, y4), (NZ - 1, z4),
+        (NY - 1, y1(0)), (NY - 1, y1(1)), (NZ - 1, z2), (NY - 1, y2), (NZ - 1, z3), (NY - 1, y3), (NY - 1, y4),
     ):
         sent(count, make)
     for d in range(NX):
         gram_core(d).wait_send()
+    for way in range(2):
+        for number in range(4):
+            z_sum(number, way).wait_send()
+            z_all(number, way).wait_send()
     for copy in outs:
         copy.wait()
 
@@ -472,13 +519,15 @@
             pltpu.VMEM((NY - 1, TY, 128, B), F32),
             pltpu.VMEM((TY, 128, B), F32),
             pltpu.VMEM((NZ - 1, TY, 16, B), F32),
-            pltpu.VMEM((NZ - 1, tz, 64, B), F32),
+            pltpu.VMEM((2, tz // 2, 64, B), F32),
+            *[pltpu.VMEM((3, tz, 64, B), F32)] * 4,
             pltpu.VMEM((tz, 64, B), F32),
             pltpu.VMEM((NY - 1, tz, 16, B), F32),
             dma((NCH,)),
             dma((NCH,)), dma((NCH,)), dma((NCH,)), dma((NCH,)),
             *y_pair, *z_pair, *z_pair, *x_pair, dma((NX,)), dma((NX,)),
-            dma((TY // 2, NY - 1)), dma((TY // 2, NY - 1)), *z_pair, *z_pair, *y_pair, *z_pair, *y_pair, *y_pair, *z_pair,
+            dma((TY // 2, NY - 1)), dma((TY // 2, NY - 1)), dma((2, 4)), dma((2, 4)),
+            *z_pair, *y_pair, *z_pair, *y_pair, *y_pair, dma((2, 4)), dma((2, 4)),
             dma((3,)),
         ],
         compiler_params=pltpu.CompilerParams(

time: 120 us -> 104 us (0.87); the launches traced: 118 us -> 104 us
  Pallas kernels: 118 us -> 103 us
    pallas_call x1, Pallas kernels: 107 us -> 93.1 us  [gather_products(): pl.pallas_call(gather_kernel, out_shape=(jax.ShapeDtypeStruct((4, ROWS, B...]
where the time goes in v3:
time: 104 us
  Pallas kernels  103 us (99%)
    pallas_call x1, Pallas kernels, gather_products(): pl.pallas_call(gather_kernel, out_shape=(jax.ShapeDtypeStruct((4, ROWS, B...  93.1 us
    pallas_call x1, Pallas kernels, project(): pl.pallas_call(project_kernel, grid=(steps,), out_shape=(jax.ShapeDtypeSt...  10.2 us

profile of v3, /device:TPU:1, one launch (start us, length us, event | category | flops | bytes accessed | tf_op | source)
XLA Modules:
  0.0 104.0 jit_solution(3681288995011010047)
XLA Ops:
  0.6 0.0 copy-start
  0.6 93.1 %gather_products.1 = (f32[4,1024,128]{2,1,0:T(8,128)S(1)}, f32[512,512]{1,0:T(8,128)S(1)}, f32[8,512,128]{2,1,0:T(8,128)S(1)}) custom-call(f32[8192,128]{1,0:T(8,128)} %bitcast.8), custom_call_target="tpu_custom_call" | custom-call | tf_op jit(solution)/shard_map/gather_products/pallas_call | solution.py:496
  93.7 0.0 copy-done
  93.7 10.2 %project.1 = (f32[4096,128]{1,0:T(8,128)}, f32[4096,128]{1,0:T(8,128)}, f32[8192,128]{1,0:T(8,128)}) custom-call(f32[8192,128]{1,0:T(8,128)S(1)} %bitcast.9, f32[4,1024,128]{2,1,0:T(8,128)S(1)} %get-tuple-element.9.p_ref, f32[512,512]{1,0:T(8,128)S(1)} %get-tuple-element.10.m_ref, f32[8,512,128]{2,1,0:T(8,128)S(1)} %get-tuple-element.11.g_ref), custom_call_target="tpu_custom_call" | custom-call | tf_op jit(solution)/shard_map/project/pallas_call | solution.py:571
Async XLA Ops:
  0.6 93.1 %copy-start = (f32[1024,4,1,256]{3,2,1,0:T(1,128)S(1)}, f32[1024,4,1,256]{3,2,1,0:T(1,128)}, u32[]{:S(2)}) copy-start(f32[1024,4,1,256]{3,2,1,0:T(1,128)} %param.1) | copy-start | bytes 12582916

commit v4 on v3

--- a/solution.py
+++ b/solution.py
@@ -44,14 +44,14 @@
 def lane_bcast(x, c):
     return jnp.broadcast_to(x[:, c:c + 1], x.shape)
 
-def leaf(x_ref, hook):
+def leaf(x_ref, hooks):
     n = B // GR
     lane = lax.broadcasted_iota(jnp.int32, (GR, B), 1)
     sub = lax.broadcasted_iota(jnp.int32, (GR, B), 0)
     x = [x_ref[GR * t:GR * (t + 1), :] for t in range(n)]
     for g in range(n):
-        if hook is not None and g == n // 2:
-            hook()
+        if g in hooks:
+            hooks[g]()
         base = GR * g
         cur = x[g]
         v = [lane_bcast(cur, base + c) for c in range(GR)]
@@ -82,11 +82,11 @@
     for t in range(n):
         x_ref[GR * t:GR * (t + 1), :] = x[t]
 
-def factor_step(k, m_ref, d_ref, hook=None):
+def factor_step(k, m_ref, d_ref, hooks):
     size = m_ref.shape[0]
     sl = slice(B * k, B * (k + 1))
     d_ref[...] = m_ref[sl, sl]
-    leaf(d_ref, hook)
+    leaf(d_ref, hooks)
     ri = lax.broadcasted_iota(jnp.int32, (B, B), 0)
     ci = lax.broadcasted_iota(jnp.int32, (B, B), 1)
     m = jnp.where(ri >= ci, d_ref[...], 0.0)
@@ -250,11 +250,14 @@
     for h in range(2):
         gs[h] = dot(left, pt[2 * core + h], ((0,), (0,)))
 
-    def gram_y(d):
-        return remote(gs, gy.at[y], gy_s.at[d - 1], gy_r.at[d - 1], at_y(d))
-
-    exchange(NY - 1, gram_y)
-    gy[y] = gs[...]
+    def rows16(ref, index):
+        return ref.at[:, pl.ds(pl.multiple_of(index * 16, 16), 16), :]
+
+    def gram_z(d):
+        return remote(rows16(gs, (z + d) % NZ), gz.at[z], gz_s.at[d - 1], gz_r.at[d - 1], at_z(d))
+
+    exchange(NZ - 1, gram_z)
+    gz[z] = gs[:, pl.ds(pl.multiple_of(z * 16, 16), 16), :]
 
     for q in range(4):
         high, low = split(pt[q])
@@ -314,36 +317,50 @@
     z_hop(0)
     local_products(0)
     exchange(NY - 1, y1(0))
+
+    def z2(pair):
+        lo = 2 * pair
+
+        def make(d):
+            src = rows_of(sy, lo, lo + 2, (z + d) % NZ, 16)
+            return remote(src, rz2.at[d - 1, lo : lo + 2], z2_s.at[pair, d - 1], z2_r.at[pair, d - 1], at_z(d))
+
+        return make
+
+    def add_y(pair):
+        part = slice(2 * pair, 2 * pair + 2)
+        arrived(NY - 1, y1(pair))
+        own = gl[part, pl.ds(pl.multiple_of(y * 128, 128), 128), :]
+        sy[part] = (own + ry[0, part]) + (ry[1, part] + ry[2, part])
+        exchange(NZ - 1, z2(pair))
+
+    arrived(NZ - 1, gram_z)
+    total = gz[0]
+    for i in range(1, NZ):
+        total = total + gz[i]
+    gsum[...] = total
+
+    def gram_y(d):
+        return remote(gsum, gy.at[y], gy_s.at[d - 1], gy_r.at[d - 1], at_y(d))
+
+    exchange(NY - 1, gram_y)
+    gy[y] = gsum[...]
     z_hop(1)
     local_products(2)
     exchange(NY - 1, y1(1))
     arrived(NY - 1, gram_y)
-    gsum[...] = (gy[0] + gy[1]) + (gy[2] + gy[3])
-
-    def rows16(ref, index):
-        return ref.at[:, pl.ds(pl.multiple_of(index * 16, 16), 16), :]
-
-    def gram_z(d):
-        return remote(rows16(gsum, (z + d) % NZ), gz.at[z], gz_s.at[d - 1], gz_r.at[d - 1], at_z(d))
-
-    exchange(NZ - 1, gram_z)
-    gz[z] = gsum[:, pl.ds(pl.multiple_of(z * 16, 16), 16), :]
-    z_hop(2)
-    arrived(NZ - 1, gram_z)
 
     def gram_piece():
         return gram.at[x, pl.ds(2 * core, 2), pl.ds(pl.multiple_of(z * 16, 16), 16), :]
 
-    total = gz[0]
-    for i in range(1, NZ):
-        total = total + gz[i]
-    gram[x, pl.ds(2 * core, 2), pl.ds(pl.multiple_of(z * 16, 16), 16), :] = total
+    gram[x, pl.ds(2 * core, 2), pl.ds(pl.multiple_of(z * 16, 16), 16), :] = (gy[0] + gy[1]) + (gy[2] + gy[3])
 
     def gram_all(d):
         return remote(gram_piece(), gram_piece(), ga_s.at[d - 1], ga_r.at[d - 1], at_z(d))
 
     exchange(NZ - 1, gram_all)
-    z_hop(3)
+    z_hop(2)
+    add_y(0)
     arrived(NZ - 1, gram_all)
 
     def gram_block(index):
@@ -363,14 +380,8 @@
         gram_x(d).wait_recv()
         gram_core(d).start()
 
-    for pair in range(TY // 2):
-        arrived(NY - 1, y1(pair))
-    sy[...] = (gl[0:TY, pl.ds(pl.multiple_of(y * 128, 128), 128), :] + ry[0]) + (ry[1] + ry[2])
-
-    def z2(d):
-        return remote(rows_of(sy, 0, TY, (z + d) % NZ, 16), rz2.at[d - 1], z2_s.at[d - 1], z2_r.at[d - 1], at_z(d))
-
-    exchange(NZ - 1, z2)
+    z_hop(3)
+    add_y(1)
     for way in range(2):
         z_sum(3, way).wait_recv()
     sz[...] = block(TY, TILES, z) + (in_r[2] + in_l[2])
@@ -386,34 +397,37 @@
     for k in range(4):
         for t in range(4):
             mm[B * k : B * (k + 1), B * t : B * (t + 1)] = gram[k, t] if t >= k else jnp.zeros((B, B), F32)
-    factor_step(0, mm, dd)
-
-    arrived(NZ - 1, z2)
-    total = sy[:, pl.ds(pl.multiple_of(z * 16, 16), 16), :]
-    for i in range(NZ - 1):
-        total = total + rz2[i]
-    gf[0:TY, pl.ds(pl.multiple_of((y * NZ + z) * 16, 16), 16), :] = total
-
-    def z3(d):
-        piece = rows_of(gf, 0, TY, y * NZ + z, 16)
-        return remote(piece, piece, z3_s.at[d - 1], z3_r.at[d - 1], at_z(d))
-
-    exchange(NZ - 1, z3)
+    def y3(d):
+        piece = rows_of(gf, TY, TILES, z * NY + y, 16)
+        return remote(piece, piece, y3_s.at[d - 1], y3_r.at[d - 1], at_y(d))
+
     arrived(NY - 1, y2)
     total = sz[:, pl.ds(pl.multiple_of(y * 16, 16), 16), :]
     for i in range(NY - 1):
         total = total + ry2[i]
     gf[TY:TILES, pl.ds(pl.multiple_of((z * NY + y) * 16, 16), 16), :] = total
-
-    def y3(d):
-        piece = rows_of(gf, TY, TILES, z * NY + y, 16)
-        return remote(piece, piece, y3_s.at[d - 1], y3_r.at[d - 1], at_y(d))
-
     exchange(NY - 1, y3)
 
-    def y4(d):
-        piece = rows_of(gf, 0, TY, y, 128)
-        return remote(piece, piece, y4_s.at[d - 1], y4_r.at[d - 1], at_y(d))
+    def z3(d):
+        piece = rows_of(gf, 0, TY, y * NZ + z, 16)
+        return remote(piece, piece, z3_s.at[d - 1], z3_r.at[d - 1], at_z(d))
+
+    def y4(source):
+        piece = rows_of(gf, 0, TY, y * NZ + (z + NZ - source) % NZ, 16)
+
+        def make(d):
+            return remote(piece, piece, y4_s.at[source, d - 1], y4_r.at[source, d - 1], at_y(d))
+
+        return make
+
+    for pair in range(TY // 2):
+        arrived(NZ - 1, z2(pair))
+    total = sy[:, pl.ds(pl.multiple_of(z * 16, 16), 16), :]
+    for i in range(NZ - 1):
+        total = total + rz2[i]
+    gf[0:TY, pl.ds(pl.multiple_of((y * NZ + z) * 16, 16), 16), :] = total
+    exchange(NZ - 1, z3)
+    exchange(NY - 1, y4(0))
 
     def z_all(hop, way):
         to = ways[way][0]
@@ -434,14 +448,15 @@
         arrived(NY - 1, y3)
         hop(0)
 
-    factor_step(1, mm, dd, begin)
-    arrived(NZ - 1, z3)
-    exchange(NY - 1, y4)
-    hop(1)
-    factor_step(2, mm, dd, lambda: hop(2))
-    hop(3)
-    factor_step(3, mm, dd)
-    arrived(NY - 1, y4)
+    def forward(d):
+        z3(d).wait_recv()
+        exchange(NY - 1, y4(d))
+
+    factor_step(0, mm, dd, {4: begin, 13: lambda: each(NZ - 1, forward)})
+    factor_step(1, mm, dd, {3: lambda: hop(1)})
+    factor_step(2, mm, dd, {2: lambda: hop(2)})
+    factor_step(3, mm, dd, {1: lambda: hop(3)})
+    loop(NZ, lambda source: arrived(NY - 1, y4(source)))
     for way in range(2):
         z_all(3, way).wait_recv()
 
@@ -473,11 +488,12 @@
     loop(NCH, lambda i: across(i).wait_send())
     for count, make in (
         (NY - 1, gram_y), (NZ - 1, gram_z), (NZ - 1, gram_all), (NX - 1, gram_x),
-        (NY - 1, y1(0)), (NY - 1, y1(1)), (NZ - 1, z2), (NY - 1, y2), (NZ - 1, z3), (NY - 1, y3), (NY - 1, y4),
+        (NY - 1, y1(0)), (NY - 1, y1(1)), (NZ - 1, z2(0)), (NZ - 1, z2(1)), (NY - 1, y2), (NZ - 1, z3), (NY - 1, y3),
     ):
         sent(count, make)
     for d in range(NX):
         gram_core(d).wait_send()
+    loop(NZ, lambda source: sent(NY - 1, y4(source)))
     for way in range(2):
         for number in range(4):
             z_sum(number, way).wait_send()
@@ -510,8 +526,8 @@
             pltpu.VMEM((WIDTH, WIDTH), F32),
             pltpu.VMEM((B, B), F32),
             pltpu.VMEM((2, B, B), F32),
-            pltpu.VMEM((NY, 2, B, B), F32),
-            pltpu.VMEM((2, B, B), F32),
+            pltpu.VMEM((NY, 2, 16, B), F32),
+            pltpu.VMEM((2, 16, B), F32),
             pltpu.VMEM((NZ, 2, 16, B), F32),
             pltpu.VMEM((4, 4, B, B), F32),
             pltpu.VMEM((TILES, WIDTH, B), F32),
@@ -527,7 +543,8 @@
             dma((NCH,)), dma((NCH,)), dma((NCH,)), dma((NCH,)),
             *y_pair, *z_pair, *z_pair, *x_pair, dma((NX,)), dma((NX,)),
             dma((TY // 2, NY - 1)), dma((TY // 2, NY - 1)), dma((2, 4)), dma((2, 4)),
-            *z_pair, *y_pair, *z_pair, *y_pair, *y_pair, dma((2, 4)), dma((2, 4)),
+            dma((TY // 2, NZ - 1)), dma((TY // 2, NZ - 1)), *y_pair, *z_pair, *y_pair, dma((NZ, NY - 1)), dma((NZ, NY - 1)),
+            dma((2, 4)), dma((2, 4)),
             dma((3,)),
         ],
         compiler_params=pltpu.CompilerParams(
@@ -537,58 +554,65 @@
     )(flat)
 
 
-def project_kernel(a_ref, p_ref, m_ref, g_ref, rows_ref, basis_ref, trail_ref, wh, wl):
-    rows = p_ref.shape[1]
+def project_kernel(a_ref, p_ref, m_ref, g_ref, rows_hbm, basis_hbm, trail_hbm, wh, wl, rows_out, basis_out, trail_out, sems):
     inverse = split(m_ref[...])
     half = WIDTH // 2
-
-    @pl.when(pl.program_id(0) == 0)
-    def _():
-        for t in range(0, TILES, 2):
-            g = split(jnp.concatenate([g_ref[t], g_ref[t + 1]], axis=1))
-            upper = dot3([v[:half, :half] for v in inverse], [v[:half] for v in g], ((1,), (0,)))
-            lower = dot3([v[half:] for v in inverse], g, ((1,), (0,)))
-            w = jnp.concatenate([upper, lower], axis=0)
-            for h in range(2):
-                rows_ref[pl.ds(t + h, WIDTH, stride=TILES), :] = w[:, B * h : B * (h + 1)]
-            wh[t // 2], wl[t // 2] = split(w)
-
-    panel = split(jnp.concatenate([p_ref[q] for q in range(4)], axis=1))
-    basis = dot3(panel, inverse, ((1,), (1,)))
-    for q in range(4):
-        basis_ref[pl.ds((q % 2) * 2 + q // 2, rows, stride=4), :] = basis[:, B * q : B * (q + 1)]
-    pair = split(basis)
-    for t in range(0, TILES, 2):
-        part = dot3(pair, (wh[t // 2], wl[t // 2]), ((1,), (0,)))
-        for h in range(2):
-            spot = pl.ds(t + h, rows, stride=TILES)
-            trail_ref[spot, :] = a_ref[spot, :] - part[:, B * h : B * (h + 1)]
-
-
-def project(flat, panels, inverse, products):
     steps = 4
     rows = ROWS // steps
+
+    def store(src, dst, size, index, sem):
+        part = pl.ds(size * index, size)
+        return pltpu.make_async_copy(src.at[part, :], dst.at[part, :], sem)
+
+    copies = []
+
+    def send(*args):
+        copies.append(store(*args, sems.at[len(copies)]))
+        copies[-1].start()
+
+    pairs = []
+    for i in range(steps):
+        panel = split(jnp.concatenate([p_ref[q, rows * i : rows * (i + 1), :] for q in range(4)], axis=1))
+        basis = dot3(panel, inverse, ((1,), (1,)))
+        for q in range(4):
+            basis_out[pl.ds(4 * rows * i + (q % 2) * 2 + q // 2, rows, stride=4), :] = basis[:, B * q : B * (q + 1)]
+        bh, bl = split(basis)
+        pairs.append((bh, bl))
+        send(basis_out, basis_hbm, 4 * rows, i)
+    for t in range(0, TILES, 2):
+        g = split(jnp.concatenate([g_ref[t], g_ref[t + 1]], axis=1))
+        upper = dot3([v[:half, :half] for v in inverse], [v[:half] for v in g], ((1,), (0,)))
+        lower = dot3([v[half:] for v in inverse], g, ((1,), (0,)))
+        w = jnp.concatenate([upper, lower], axis=0)
+        for h in range(2):
+            rows_out[pl.ds(t + h, WIDTH, stride=TILES), :] = w[:, B * h : B * (h + 1)]
+        wh[t // 2], wl[t // 2] = split(w)
+    send(rows_out, rows_hbm, WIDTH * TILES, 0)
+    for i in range(steps):
+        for t in range(0, TILES, 2):
+            part = dot3(pairs[i], (wh[t // 2], wl[t // 2]), ((1,), (0,)))
+            for h in range(2):
+                spot = pl.ds(TILES * rows * i + t + h, rows, stride=TILES)
+                trail_out[spot, :] = a_ref[spot, :] - part[:, B * h : B * (h + 1)]
+        send(trail_out, trail_hbm, TILES * rows, i)
+    for copy in copies:
+        copy.wait()
+
+
+def project(flat, panels, inverse, products):
+    any_space = pl.BlockSpec(memory_space=pl.ANY)
+    shapes = ((WIDTH * TILES, B), (ROWS * 4, B), (ROWS * TILES, B))
     return pl.pallas_call(
         project_kernel,
-        grid=(steps,),
-        out_shape=(
-            jax.ShapeDtypeStruct((WIDTH * TILES, B), F32),
-            jax.ShapeDtypeStruct((ROWS * 4, B), F32),
-            jax.ShapeDtypeStruct((ROWS * TILES, B), F32),
-        ),
-        in_specs=[
-            pl.BlockSpec((rows * TILES, B), lambda i: (i, 0)),
-            pl.BlockSpec((4, rows, B), lambda i: (0, i, 0)),
-            pl.BlockSpec((WIDTH, WIDTH), lambda i: (0, 0)),
-            pl.BlockSpec((TILES, WIDTH, B), lambda i: (0, 0, 0)),
+        out_shape=tuple(jax.ShapeDtypeStruct(shape, F32) for shape in shapes),
+        in_specs=[pl.BlockSpec(memory_space=pltpu.VMEM)] * 4,
+        out_specs=(any_space,) * 3,
+        scratch_shapes=[
+            *[pltpu.VMEM((TILES // 2, WIDTH, 2 * B), BF16)] * 2,
+            *[pltpu.VMEM(shape, F32) for shape in shapes],
+            pltpu.SemaphoreType.DMA((9,)),
         ],
-        out_specs=(
-            pl.BlockSpec((WIDTH * TILES, B), lambda i: (0, 0)),
-            pl.BlockSpec((rows * 4, B), lambda i: (i, 0)),
-            pl.BlockSpec((rows * TILES, B), lambda i: (i, 0)),
-        ),
-        scratch_shapes=[pltpu.VMEM((TILES // 2, WIDTH, 2 * B), BF16)] * 2,
-        compiler_params=pltpu.CompilerParams(vmem_limit_bytes=40 << 20),
+        compiler_params=pltpu.CompilerParams(vmem_limit_bytes=32 << 20),
         name="project",
     )(flat, panels, inverse, products)
 

time: 104 us -> 99.9 us (0.961); the launches traced: 104 us -> 98.5 us
  Pallas kernels: 103 us -> 97.7 us
    pallas_call x1, Pallas kernels: 93.1 us -> 89.3 us  [gather_products(): pl.pallas_call(gather_kernel, out_shape=(jax.ShapeDtypeStruct((4, ROWS, B...]
    pallas_call x1, Pallas kernels: 10.2 us -> 8.33 us  [project(): pl.pallas_call(project_kernel, out_shape=tuple((jax.ShapeDtypeStruct(shap...]
where the time goes in v4:
time: 99.9 us; the launch traced here: 98.5 us
  Pallas kernels  97.7 us (98%)
    pallas_call x1, Pallas kernels, gather_products(): pl.pallas_call(gather_kernel, out_shape=(jax.ShapeDtypeStruct((4, ROWS, B...  89.3 us
    pallas_call x1, Pallas kernels, project(): pl.pallas_call(project_kernel, out_shape=tuple((jax.ShapeDtypeStruct(shap...  8.33 us

profile of v4, /device:TPU:1, one launch (start us, length us, event | category | flops | bytes accessed | tf_op | source)
XLA Modules:
  0.0 98.5 jit_solution(1604949953549730034)
XLA Ops:
  0.6 0.0 copy-start
  0.6 89.3 %gather_products.1 = (f32[4,1024,128]{2,1,0:T(8,128)S(1)}, f32[512,512]{1,0:T(8,128)S(1)}, f32[8,512,128]{2,1,0:T(8,128)S(1)}) custom-call(f32[8192,128]{1,0:T(8,128)} %bitcast.8), custom_call_target="tpu_custom_call" | custom-call | tf_op jit(solution)/shard_map/gather_products/pallas_call | solution.py:512
  90.0 0.0 copy-done
  90.0 8.3 %project.1 = (f32[4096,128]{1,0:T(8,128)}, f32[4096,128]{1,0:T(8,128)}, f32[8192,128]{1,0:T(8,128)}) custom-call(f32[8192,128]{1,0:T(8,128)S(1)} %bitcast.9, f32[4,1024,128]{2,1,0:T(8,128)S(1)} %get-tuple-element.9.p_ref, f32[512,512]{1,0:T(8,128)S(1)} %get-tuple-element.10.m_ref, f32[8,512,128]{2,1,0:T(8,128)S(1)} %get-tuple-element.11.g_ref), custom_call_target="tpu_custom_call" | custom-call | tf_op jit(solution)/shard_map/project/pallas_call | solution.py:605
Async XLA Ops:
  0.6 89.3 %copy-start = (f32[1024,4,1,256]{3,2,1,0:T(1,128)S(1)}, f32[1024,4,1,256]{3,2,1,0:T(1,128)}, u32[]{:S(2)}) copy-start(f32[1024,4,1,256]{3,2,1,0:T(1,128)} %param.1) | copy-start | bytes 12582916

commit v5 on v4

--- a/solution.py
+++ b/solution.py
@@ -429,20 +429,21 @@
     exchange(NZ - 1, z3)
     exchange(NY - 1, y4(0))
 
-    def z_all(hop, way):
+    def z_all(hop, way, part):
         to = ways[way][0]
         index = (z + NZ - hop) % NZ if way == 0 else (z + hop) % NZ
-        lo, hi = TY, TILES
-        if hop == 3:
-            lo, hi = (TY, near) if way == 0 else (near, TILES)
+        lo, hi = (TY, near) if part == 0 else (near, TILES)
         piece = rows_of(gf, lo, hi, index, 64)
-        return remote(piece, piece, all_s.at[way, hop], all_r.at[way, hop], at_z(to))
+        return remote(piece, piece, all_s.at[way, hop, part], all_r.at[way, hop, part], at_z(to))
+
+    legs = [(number, way, part) for number in range(4) for part in range(2) for way in range(2) if number < 3 or part == way]
 
     def hop(number):
-        for way in range(2):
-            if number:
-                z_all(number - 1, way).wait_recv()
-            z_all(number, way).start()
+        for leg in legs:
+            if leg[0] == number:
+                if number:
+                    z_all(number - 1, *leg[1:]).wait_recv()
+                z_all(*leg).start()
 
     def begin():
         arrived(NY - 1, y3)
@@ -457,8 +458,9 @@
     factor_step(2, mm, dd, {2: lambda: hop(2)})
     factor_step(3, mm, dd, {1: lambda: hop(3)})
     loop(NZ, lambda source: arrived(NY - 1, y4(source)))
-    for way in range(2):
-        z_all(3, way).wait_recv()
+    for number, way, part in legs:
+        if number == 3 or (number == 2 and part != way):
+            z_all(number, way, part).wait_recv()
 
     outs = [
         pltpu.make_async_copy(src, dst, out_sem.at[i])
@@ -497,7 +499,8 @@
     for way in range(2):
         for number in range(4):
             z_sum(number, way).wait_send()
-            z_all(number, way).wait_send()
+    for leg in legs:
+        z_all(*leg).wait_send()
     for copy in outs:
         copy.wait()
 
@@ -544,7 +547,7 @@
             *y_pair, *z_pair, *z_pair, *x_pair, dma((NX,)), dma((NX,)),
             dma((TY // 2, NY - 1)), dma((TY // 2, NY - 1)), dma((2, 4)), dma((2, 4)),
             dma((TY // 2, NZ - 1)), dma((TY // 2, NZ - 1)), *y_pair, *z_pair, *y_pair, dma((NZ, NY - 1)), dma((NZ, NY - 1)),
-            dma((2, 4)), dma((2, 4)),
+            dma((2, 4, 2)), dma((2, 4, 2)),
             dma((3,)),
         ],
         compiler_params=pltpu.CompilerParams(

time: 99.9 us -> 99.3 us (level)
  no operation moved by 1% of the time
where the time goes in v5:
time: 99.3 us; the launch traced here: 98.4 us
  Pallas kernels  97.5 us (98%)
    pallas_call x1, Pallas kernels, gather_products(): pl.pallas_call(gather_kernel, out_shape=(jax.ShapeDtypeStruct((4, ROWS, B...  89.2 us
    pallas_call x1, Pallas kernels, project(): pl.pallas_call(project_kernel, out_shape=tuple((jax.ShapeDtypeStruct(shap...  8.33 us

profile of v5, /device:TPU:1, one launch (start us, length us, event | category | flops | bytes accessed | tf_op | source)
XLA Modules:
  0.0 98.4 jit_solution(6724709459049682045)
XLA Ops:
  0.6 0.0 copy-start
  0.6 89.2 %gather_products.1 = (f32[4,1024,128]{2,1,0:T(8,128)S(1)}, f32[512,512]{1,0:T(8,128)S(1)}, f32[8,512,128]{2,1,0:T(8,128)S(1)}) custom-call(f32[8192,128]{1,0:T(8,128)} %bitcast.8), custom_call_target="tpu_custom_call" | custom-call | tf_op jit(solution)/shard_map/gather_products/pallas_call | solution.py:515
  89.8 0.0 copy-done
  89.8 8.3 %project.1 = (f32[4096,128]{1,0:T(8,128)}, f32[4096,128]{1,0:T(8,128)}, f32[8192,128]{1,0:T(8,128)}) custom-call(f32[8192,128]{1,0:T(8,128)S(1)} %bitcast.9, f32[4,1024,128]{2,1,0:T(8,128)S(1)} %get-tuple-element.9.p_ref, f32[512,512]{1,0:T(8,128)S(1)} %get-tuple-element.10.m_ref, f32[8,512,128]{2,1,0:T(8,128)S(1)} %get-tuple-element.11.g_ref), custom_call_target="tpu_custom_call" | custom-call | tf_op jit(solution)/shard_map/project/pallas_call | solution.py:608
Async XLA Ops:
  0.6 89.2 %copy-start = (f32[1024,4,1,256]{3,2,1,0:T(1,128)S(1)}, f32[1024,4,1,256]{3,2,1,0:T(1,128)}, u32[]{:S(2)}) copy-start(f32[1024,4,1,256]{3,2,1,0:T(1,128)} %param.1) | copy-start | bytes 12582916
